TPU v7x, 32 devices: a whole 2x2x4 slice. The times are simulated.
32 devices in a mesh: section: 2 (over y), dp: 4 (over x, core), tensor: 4 (over z).
Axes of the slice: x: 2, y: 2, z: 4, core: 2. Of those that a mesh axis runs over, the one named last changes fastest.
Arguments:
- master_weight: float32 [2304, 128, 128], P(('section', 'tensor'), 'dp'), parts along dimension 0, may hold values from -6 to 6
- first_moment: float32 [2304, 128, 128], P(('section', 'tensor'), 'dp'), parts along dimension 0, may hold values from -2 to 2
- second_moment: float32 [2304, 128, 128], P(('section', 'tensor'), 'dp'), parts along dimension 0, may hold values from 0.01 to 1
- grads: bfloat16 [4, 2304, 128, 128], P('dp', ('section', 'tensor')), parts along dimension 1, may hold values from -6 to 6
- dest_table: int32 [1152], replicated, may hold values from 0 to 1151, as said below
Outputs:
- weight_new: float32 [2304, 128, 128], P(('section', 'tensor'), 'dp'), parts along dimension 0
- first_new: float32 [2304, 128, 128], P(('section', 'tensor'), 'dp'), parts along dimension 0
- second_new: float32 [2304, 128, 128], P(('section', 'tensor'), 'dp'), parts along dimension 0
- weights: bfloat16 [2304, 128, 128], P(('section', 'tensor')), parts along dimension 0
There are 2 independent parts, one for each index of `section`. A program takes and returns all parts, laid end to end along the dimension named above; an argument that names none is the same for every part. Nothing has to cross between parts.
Inputs may be any that keep to these rules, and one draw needn't show every extreme that they name: `dest_table`: A permutation. Group old slots by s // 288 and new positions by p // 288: at most 72 slots of one group have positions in one block, and some pair of group and block has exactly 72.
All inputs are finite; a program needn't handle non-finite values.
Results may differ from a plain program's by a relative error of at most 0.0023.
Values may be sent and summed in bfloat16 or wider, within the bound.
A program may use at most 128 MiB of HBM per device.

v0:
```python
import functools

import jax
import jax.numpy as jnp
from jax import lax
from jax.experimental import pallas as pl
from jax.experimental.pallas import tpu as pltpu
from jax.sharding import PartitionSpec as P

STEP = 10


learn_rate = 0.04
decay_rate = 1.5
beta_first = 0.9
beta_second = 0.95
epsilon = 1e-08


def adam_step(weight, first, second, grad):
    first_new = beta_first * first + (1.0 - beta_first) * grad
    second_new = beta_second * second + (1.0 - beta_second) * grad * grad
    first_hat = first_new / (1.0 - beta_first**STEP)
    second_hat = second_new / (1.0 - beta_second**STEP)
    weight_new = weight - learn_rate * (
        first_hat / (jnp.sqrt(second_hat) + epsilon) + decay_rate * weight
    )
    return (weight_new, first_new, second_new)


def routes(dest_table, slots, groups, capacity, rank_here):
    total = dest_table.shape[0]
    length = groups * capacity
    target = dest_table // slots
    local = dest_table % slots
    layout = target.reshape(groups, slots)
    order = jnp.arange(slots, dtype=jnp.int32)
    same = (layout[:, :, None] == layout[:, None, :]) & (order[None, :] < order[:, None])[None]
    within = jnp.sum(same.astype(jnp.int32), axis=2).reshape(total)
    source = jnp.arange(total, dtype=jnp.int32) // slots
    leaving = lax.dynamic_slice_in_dim(target * capacity + within, rank_here * slots, slots)
    places = jnp.arange(length, dtype=jnp.int32)
    outgoing = jnp.sum(jnp.where(leaving[None, :] == places[:, None], order[None, :], 0), axis=1)
    landing = jnp.where(target == rank_here, local, slots)
    incoming = jnp.sum(
        jnp.where(landing[None, :] == order[:, None], (source * capacity + within)[None, :], 0),
        axis=1,
    )
    return (outgoing, incoming)


ROWS = 8
SCALE = 8192.0
SPARE = 256 * 1024
MESH = pl.DeviceIdType.MESH


def encode(weight):
    scaled = weight * SCALE
    square = scaled * scaled
    fourth = square * square
    return (scaled * jnp.abs(scaled) * square * fourth).astype(jnp.bfloat16)


def decode(code):
    wide = code.astype(jnp.float32)
    root = jnp.sqrt(jnp.sqrt(jnp.sqrt(jnp.abs(wide)))) * (1.0 / SCALE)
    return jnp.where(wide < 0.0, -root, root)


def exchange_kernel(
    groups, replicas, capacity, chunks,
    outgoing, incoming, weight, first, second, grads,
    weight_new, first_new, second_new, weights,
    raw, sent, got, got_grads, rounded,
    load_sem, out_sem, own_sem, wide_send, wide_recv, grad_own, grad_send, grad_recv,
    last_own, last_send, last_recv, relay_send,
):
    slots, rows = weight.shape[0], weight.shape[1]
    length = groups * capacity
    me = lax.axis_index("tensor")
    mine = lax.axis_index("dp")
    hops = sorted(range(1, groups), key=lambda k: -min(k, groups - k))
    turns = range(1, replicas)

    def band(chunk, owner=None):
        start = chunk * ROWS if owner is None else owner * rows + chunk * ROWS
        return pl.ds(start, ROWS)

    def loads(chunk):
        return [
            pltpu.make_async_copy(
                ref.at[:, band(chunk), :], raw[chunk % 2].at[k], load_sem.at[chunk % 2, k]
            )
            for k, ref in enumerate((weight, first, second))
        ]

    def wide(chunk, source, target):
        return pltpu.make_async_remote_copy(
            src_ref=sent.at[chunk, :, pl.ds(target * capacity, capacity)],
            dst_ref=got[chunk].at[:, pl.ds(source * capacity, capacity)],
            send_sem=wide_send.at[chunk, target],
            recv_sem=wide_recv.at[chunk, source],
            device_id={"tensor": target},
            device_id_type=MESH,
        )

    def own(chunk):
        here = pl.ds(me * capacity, capacity)
        return pltpu.make_async_copy(
            sent.at[chunk, :, here], got[chunk].at[:, here], own_sem.at[chunk]
        )

    def grad_copy(chunk, source, target):
        return pltpu.make_async_remote_copy(
            src_ref=grads.at[0, :, band(chunk, target), :],
            dst_ref=got_grads.at[source, chunk],
            send_sem=grad_send.at[chunk, target],
            recv_sem=grad_recv.at[chunk, source],
            device_id={"dp": target},
            device_id_type=MESH,
        )

    def grad_here(chunk):
        return pltpu.make_async_copy(
            grads.at[0, :, band(chunk, mine), :], got_grads.at[mine, chunk], grad_own.at[chunk]
        )

    def last_copy(chunk, source, target):
        return pltpu.make_async_remote_copy(
            src_ref=rounded.at[chunk],
            dst_ref=weights.at[:, band(chunk, source), :],
            send_sem=last_send.at[chunk, target],
            recv_sem=last_recv.at[chunk, source],
            device_id={"dp": target},
            device_id_type=MESH,
        )

    def relay(chunk, source):
        rows_there = weights.at[:, band(chunk, source), :]
        return pltpu.make_async_remote_copy(
            src_ref=rows_there,
            dst_ref=rows_there,
            send_sem=relay_send.at[chunk, source],
            recv_sem=last_recv.at[chunk, source],
            device_id={"dp": twin},
            device_id_type=MESH,
        )

    def last_here(chunk):
        return pltpu.make_async_copy(
            rounded.at[chunk], weights.at[:, band(chunk, mine), :], last_own.at[chunk]
        )

    def stores(chunk):
        return [
            pltpu.make_async_copy(
                raw[chunk % 2].at[k], ref.at[:, band(chunk), :], out_sem.at[chunk % 2, k]
            )
            for k, ref in enumerate((weight_new, first_new, second_new))
        ]

    def start(copies):
        for copy in copies:
            copy.start()

    def finish(copies):
        for copy in copies:
            copy.wait()

    def partner(k):
        return lax.rem(me + k, groups)

    def peer(k):
        return lax.rem(mine + k, replicas)

    core = lax.rem(mine, 2)
    twin = mine + 1 - 2 * core
    across = range(1, replicas // 2)

    def far(k):
        return lax.rem(mine + 2 * k, replicas)

    def far_twin(k):
        return lax.rem(mine + 2 * k, replicas) + 1 - 2 * core

    start(loads(0))
    if chunks > 1:
        start(loads(1))
    barrier = pltpu.get_barrier_semaphore()
    for k in hops:
        pl.semaphore_signal(barrier, inc=1, device_id={"tensor": partner(k)}, device_id_type=MESH)
    for k in turns:
        pl.semaphore_signal(barrier, inc=1, device_id={"dp": peer(k)}, device_id_type=MESH)
    pl.semaphore_wait(barrier, groups - 1 + replicas - 1)

    for chunk in range(chunks):
        finish(loads(chunk))

        def pack(j, carry, chunk=chunk):
            s = outgoing[j]
            sent[chunk, 0, j] = encode(raw[chunk % 2][0, s])
            sent[chunk, 1, j] = raw[chunk % 2][1, s].astype(jnp.bfloat16)
            sent[chunk, 2, j] = raw[chunk % 2][2, s].astype(jnp.bfloat16)
            return carry

        lax.fori_loop(0, length, pack, 0, unroll=8)
        if chunk + 2 < chunks:
            start(loads(chunk + 2))
        start([wide(chunk, me, partner(k)) for k in hops])
        own(chunk).start()
        start([grad_copy(chunk, mine, peer(k)) for k in turns])
        grad_here(chunk).start()

    for chunk in range(chunks):
        grad_here(chunk).wait()
        for k in turns:
            grad_copy(chunk, peer(k), mine).wait_recv()
        own(chunk).wait()
        for k in hops:
            wide(chunk, partner(k), me).wait_recv()
        if chunk >= 2:
            finish(stores(chunk - 2))

        def update(p, carry, chunk=chunk):
            j = incoming[p]
            grad = got_grads[0, chunk, p].astype(jnp.float32)
            for r in range(1, replicas):
                grad = grad + got_grads[r, chunk, p].astype(jnp.float32)
            weight_here, first_here, second_here = adam_step(
                decode(got[chunk][0, j]),
                got[chunk][1, j].astype(jnp.float32),
                got[chunk][2, j].astype(jnp.float32),
                grad / replicas,
            )
            rounded[chunk, p] = weight_here.astype(jnp.bfloat16)
            raw[chunk % 2][0, p] = weight_here
            raw[chunk % 2][1, p] = first_here
            raw[chunk % 2][2, p] = second_here
            return carry

        lax.fori_loop(0, slots, update, 0, unroll=4)
        start(stores(chunk))
        start([last_copy(chunk, mine, far(k)) for k in across])
        last_copy(chunk, mine, twin).start()
        last_here(chunk).start()

    for chunk in range(chunks):
        for k in across:
            last_copy(chunk, far(k), mine).wait_recv()
            relay(chunk, far(k)).start()

    for chunk in range(chunks):
        last_here(chunk).wait()
        last_copy(chunk, twin, mine).wait_recv()
        last_copy(chunk, mine, twin).wait_send()
        for k in across:
            last_copy(chunk, mine, far(k)).wait_send()
            relay(chunk, far(k)).wait_send()
            relay(chunk, far_twin(k)).wait_recv()
        for k in turns:
            grad_copy(chunk, mine, peer(k)).wait_send()
        for k in hops:
            wide(chunk, me, partner(k)).wait_send()
        if chunk >= chunks - 2:
            finish(stores(chunk))


def exchange(outgoing, incoming, weight, first, second, grads, groups, replicas, capacity):
    slots, rows, lanes = weight.shape
    chunks = rows // ROWS
    length = groups * capacity
    whole = pltpu.VMEM(weight.shape, jnp.float32)
    anywhere = pl.BlockSpec(memory_space=pl.ANY)
    table = pl.BlockSpec(memory_space=pltpu.SMEM)
    dma = pltpu.SemaphoreType.DMA
    part = slots * ROWS * lanes
    scratch = part * (24 + 2 * chunks + 2 * chunks * replicas) + 12 * chunks * length * ROWS * lanes
    return pl.pallas_call(
        functools.partial(exchange_kernel, groups, replicas, capacity, chunks),
        out_shape=(whole, whole, whole, pltpu.VMEM(grads.shape[1:], jnp.bfloat16)),
        in_specs=[table, table] + [anywhere] * 4,
        out_specs=(anywhere,) * 4,
        scratch_shapes=[
            [pltpu.VMEM((3, slots, ROWS, lanes), jnp.float32)] * 2,
            pltpu.VMEM((chunks, 3, length, ROWS, lanes), jnp.bfloat16),
            [pltpu.VMEM((3, length, ROWS, lanes), jnp.bfloat16)] * chunks,
            pltpu.VMEM((replicas, chunks, slots, ROWS, lanes), jnp.bfloat16),
            pltpu.VMEM((chunks, slots, ROWS, lanes), jnp.bfloat16),
            dma((2, 3)),
            dma((2, 3)),
            dma((chunks,)),
            dma((chunks, groups)),
            dma((chunks, groups)),
            dma((chunks,)),
            dma((chunks, replicas)),
            dma((chunks, replicas)),
            dma((chunks,)),
            dma((chunks, replicas)),
            dma((chunks, replicas)),
            dma((chunks, replicas)),
        ],
        compiler_params=pltpu.CompilerParams(
            collective_id=0, has_side_effects=True, vmem_limit_bytes=scratch + SPARE
        ),
        name="exchange",
    )(outgoing, incoming, weight, first, second, grads)


def shards(master_weight, first_moment, second_moment, grads, dest_table):
    groups = lax.axis_size("tensor")
    rank_here = lax.axis_index("tensor")
    slots = master_weight.shape[0]
    capacity = 2 * ((slots + 2 * groups - 1) // (2 * groups))
    outgoing, incoming = routes(dest_table, slots, groups, capacity, rank_here)
    replicas = lax.axis_size("dp")
    return exchange(
        outgoing, incoming, master_weight, first_moment, second_moment, grads,
        groups, replicas, capacity,
    )


def solution(mesh):
    placed = (
        P(("section", "tensor"), "dp", None),
        P(("section", "tensor"), "dp", None),
        P(("section", "tensor"), "dp", None),
        P("dp", ("section", "tensor"), None, None),
        P(),
    )
    return jax.shard_map(
        shards,
        mesh=mesh,
        in_specs=placed,
        out_specs=(
            P(("section", "tensor"), "dp", None),
            P(("section", "tensor"), "dp", None),
            P(("section", "tensor"), "dp", None),
            P(("section", "tensor"), None, None),
        ),
        check_vma=False,
    )
```

profile of v0, /device:TPU:9, one launch (start us, length us, event | category | flops | bytes accessed | tf_op | source)
XLA Modules:
  0.0 193.4 jit_solution(5197656411269382210)
XLA Ops:
  0.6 0.7 fusion.2
  1.3 0.1 eq.24
  1.5 0.6 convert_reduce_fusion
  2.1 0.1 reshape.46
  2.2 0.1 dynamic-slice_add_fusion
  2.3 0.8 select_reduce_fusion.incoming
  3.1 0.7 select_reduce_fusion.1.outgoing
  3.8 179.2 %exchange.1 = (f32[288,32,128]{2,1,0:T(8,128)S(1)}, f32[288,32,128]{2,1,0:T(8,128)S(1)}, f32[288,32,128]{2,1,0:T(8,128)S(1)}, bf16[288,128,128]{2,1,0:T(8,128)(2,1)S(1)}) custom-call(s32[288]{0:T(512)} %select_reduce_fusion.1.outgoing, s32[288]{0:T(512)} %select_reduce_fusion.incoming, f32[288,32,128]{2,1,0:T(8,128)} %weight.1, f32[288,32,128]{2,1,0:T(8,128)} %first.1, ...), custom_call_target="tpu_custom_call" | custom-call | tf_op jit(solution)/shard_map/exchange/pallas_call | solution.py:279
  183.1 2.2 %copy.13 = f32[288,32,128]{2,1,0:T(8,128)} copy(f32[288,32,128]{2,1,0:T(8,128)S(1)} %get-tuple-element.6) | data formatting | bytes 9437184
  185.3 2.2 %copy.14 = f32[288,32,128]{2,1,0:T(8,128)} copy(f32[288,32,128]{2,1,0:T(8,128)S(1)} %get-tuple-element.7) | data formatting | bytes 9437184
  187.4 2.2 %copy.15 = f32[288,32,128]{2,1,0:T(8,128)} copy(f32[288,32,128]{2,1,0:T(8,128)S(1)} %get-tuple-element.8) | data formatting | bytes 9437184
  189.6 3.7 %copy.16 = bf16[288,128,128]{2,1,0:T(8,128)(2,1)} copy(bf16[288,128,128]{2,1,0:T(8,128)(2,1)S(1)} %get-tuple-element.9) | data formatting | bytes 18874368
  (2 shorter events, 0.0 us)
where the time goes:
time: 194 us; the launch traced here: 193 us
  Pallas kernels  179 us (92%)
  local copies, waits for them, and re-layouts  10.5 us (5%)
  other arithmetic  3.03 us (2%)
    pallas_call x1, Pallas kernels, exchange(): pl.pallas_call(functools.partial(exchange_kernel, groups, replicas, capac...  179 us
    unnamed x4, local copies, waits for them, and re-layouts  10.3 us

commit v1 on v0

--- a/solution.py
+++ b/solution.py
@@ -1,4 +1,5 @@
 import functools
+import math
 
 import jax
 import jax.numpy as jnp
@@ -20,8 +21,8 @@
 def adam_step(weight, first, second, grad):
     first_new = beta_first * first + (1.0 - beta_first) * grad
     second_new = beta_second * second + (1.0 - beta_second) * grad * grad
-    first_hat = first_new / (1.0 - beta_first**STEP)
-    second_hat = second_new / (1.0 - beta_second**STEP)
+    first_hat = first_new * (1.0 / (1.0 - beta_first**STEP))
+    second_hat = second_new * (1.0 / (1.0 - beta_second**STEP))
     weight_new = weight - learn_rate * (
         first_hat / (jnp.sqrt(second_hat) + epsilon) + decay_rate * weight
     )
@@ -52,6 +53,7 @@
 ROWS = 8
 SCALE = 8192.0
 SPARE = 256 * 1024
+PARTS = 4
 MESH = pl.DeviceIdType.MESH
 
 
@@ -77,7 +79,7 @@
     last_own, last_send, last_recv, relay_send,
 ):
     slots, rows = weight.shape[0], weight.shape[1]
-    length = groups * capacity
+    parts = PARTS if slots % PARTS == 0 else 1
     me = lax.axis_index("tensor")
     mine = lax.axis_index("dp")
     hops = sorted(range(1, groups), key=lambda k: -min(k, groups - k))
@@ -86,6 +88,9 @@
     def band(chunk, owner=None):
         start = chunk * ROWS if owner is None else owner * rows + chunk * ROWS
         return pl.ds(start, ROWS)
+
+    def tiles(part):
+        return pl.ds(part * (slots // parts), slots // parts)
 
     def loads(chunk):
         return [
@@ -126,23 +131,23 @@
             grads.at[0, :, band(chunk, mine), :], got_grads.at[mine, chunk], grad_own.at[chunk]
         )
 
-    def last_copy(chunk, source, target):
+    def last_copy(chunk, part, source, target):
         return pltpu.make_async_remote_copy(
-            src_ref=rounded.at[chunk],
-            dst_ref=weights.at[:, band(chunk, source), :],
-            send_sem=last_send.at[chunk, target],
-            recv_sem=last_recv.at[chunk, source],
+            src_ref=rounded.at[chunk, tiles(part)],
+            dst_ref=weights.at[tiles(part), band(chunk, source), :],
+            send_sem=last_send.at[chunk, part, target],
+            recv_sem=last_recv.at[chunk, part, source],
             device_id={"dp": target},
             device_id_type=MESH,
         )
 
-    def relay(chunk, source):
-        rows_there = weights.at[:, band(chunk, source), :]
+    def relay(chunk, part, source):
+        rows_there = weights.at[tiles(part), band(chunk, source), :]
         return pltpu.make_async_remote_copy(
             src_ref=rows_there,
             dst_ref=rows_there,
-            send_sem=relay_send.at[chunk, source],
-            recv_sem=last_recv.at[chunk, source],
+            send_sem=relay_send.at[chunk, part, source],
+            recv_sem=last_recv.at[chunk, part, source],
             device_id={"dp": twin},
             device_id_type=MESH,
         )
@@ -197,17 +202,28 @@
     for chunk in range(chunks):
         finish(loads(chunk))
 
-        def pack(j, carry, chunk=chunk):
-            s = outgoing[j]
-            sent[chunk, 0, j] = encode(raw[chunk % 2][0, s])
-            sent[chunk, 1, j] = raw[chunk % 2][1, s].astype(jnp.bfloat16)
-            sent[chunk, 2, j] = raw[chunk % 2][2, s].astype(jnp.bfloat16)
-            return carry
-
-        lax.fori_loop(0, length, pack, 0, unroll=8)
+        def pack(target, chunk=chunk):
+            def one(i, carry):
+                j = target * capacity + i
+                s = outgoing[j]
+                sent[chunk, 0, j] = encode(raw[chunk % 2][0, s])
+                sent[chunk, 1, j] = raw[chunk % 2][1, s].astype(jnp.bfloat16)
+                sent[chunk, 2, j] = raw[chunk % 2][2, s].astype(jnp.bfloat16)
+                return carry
+
+            lax.fori_loop(0, capacity, one, 0, unroll=math.gcd(capacity, 8))
+
+        waiting = None
+        for k in hops:
+            pack(partner(k))
+            if waiting is not None:
+                waiting.start()
+            waiting = wide(chunk, me, partner(k))
+        pack(me)
+        if waiting is not None:
+            waiting.start()
         if chunk + 2 < chunks:
             start(loads(chunk + 2))
-        start([wide(chunk, me, partner(k)) for k in hops])
         own(chunk).start()
         start([grad_copy(chunk, mine, peer(k)) for k in turns])
         grad_here(chunk).start()
@@ -231,7 +247,7 @@
                 decode(got[chunk][0, j]),
                 got[chunk][1, j].astype(jnp.float32),
                 got[chunk][2, j].astype(jnp.float32),
-                grad / replicas,
+                grad * (1.0 / replicas),
             )
             rounded[chunk, p] = weight_here.astype(jnp.bfloat16)
             raw[chunk % 2][0, p] = weight_here
@@ -239,25 +255,30 @@
             raw[chunk % 2][2, p] = second_here
             return carry
 
-        lax.fori_loop(0, slots, update, 0, unroll=4)
+        size = slots // parts
+        for part in range(parts):
+            lax.fori_loop(part * size, (part + 1) * size, update, 0, unroll=math.gcd(size, 8))
+            start([last_copy(chunk, part, mine, far(k)) for k in across])
+            last_copy(chunk, part, mine, twin).start()
         start(stores(chunk))
-        start([last_copy(chunk, mine, far(k)) for k in across])
-        last_copy(chunk, mine, twin).start()
         last_here(chunk).start()
 
-    for chunk in range(chunks):
+    pieces = [(chunk, part) for chunk in range(chunks) for part in range(parts)]
+    for chunk, part in pieces:
         for k in across:
-            last_copy(chunk, far(k), mine).wait_recv()
-            relay(chunk, far(k)).start()
+            last_copy(chunk, part, far(k), mine).wait_recv()
+            relay(chunk, part, far(k)).start()
+
+    for chunk, part in pieces:
+        last_copy(chunk, part, twin, mine).wait_recv()
+        last_copy(chunk, part, mine, twin).wait_send()
+        for k in across:
+            last_copy(chunk, part, mine, far(k)).wait_send()
+            relay(chunk, part, far(k)).wait_send()
+            relay(chunk, part, far_twin(k)).wait_recv()
 
     for chunk in range(chunks):
         last_here(chunk).wait()
-        last_copy(chunk, twin, mine).wait_recv()
-        last_copy(chunk, mine, twin).wait_send()
-        for k in across:
-            last_copy(chunk, mine, far(k)).wait_send()
-            relay(chunk, far(k)).wait_send()
-            relay(chunk, far_twin(k)).wait_recv()
         for k in turns:
             grad_copy(chunk, mine, peer(k)).wait_send()
         for k in hops:
@@ -274,8 +295,9 @@
     anywhere = pl.BlockSpec(memory_space=pl.ANY)
     table = pl.BlockSpec(memory_space=pltpu.SMEM)
     dma = pltpu.SemaphoreType.DMA
-    part = slots * ROWS * lanes
-    scratch = part * (24 + 2 * chunks + 2 * chunks * replicas) + 12 * chunks * length * ROWS * lanes
+    parts = PARTS if slots % PARTS == 0 else 1
+    block = slots * ROWS * lanes
+    scratch = block * (24 + 2 * chunks + 2 * chunks * replicas) + 12 * chunks * length * ROWS * lanes
     return pl.pallas_call(
         functools.partial(exchange_kernel, groups, replicas, capacity, chunks),
         out_shape=(whole, whole, whole, pltpu.VMEM(grads.shape[1:], jnp.bfloat16)),
@@ -296,9 +318,9 @@
             dma((chunks, replicas)),
             dma((chunks, replicas)),
             dma((chunks,)),
-            dma((chunks, replicas)),
-            dma((chunks, replicas)),
-            dma((chunks, replicas)),
+            dma((chunks, parts, replicas)),
+            dma((chunks, parts, replicas)),
+            dma((chunks, parts, replicas)),
         ],
         compiler_params=pltpu.CompilerParams(
             collective_id=0, has_side_effects=True, vmem_limit_bytes=scratch + SPARE

time: 194 us -> 191 us (0.985)
  Pallas kernels: 179 us -> 176 us
    pallas_call x1, Pallas kernels: 179 us -> 176 us  [exchange(): pl.pallas_call(functools.partial(exchange_kernel, groups, replicas, capac...]
where the time goes in v1:
time: 191 us; the launch traced here: 190 us
  Pallas kernels  176 us (92%)
  local copies, waits for them, and re-layouts  10.5 us (5%)
  other arithmetic  3.03 us (2%)
    pallas_call x1, Pallas kernels, exchange(): pl.pallas_call(functools.partial(exchange_kernel, groups, replicas, capac...  176 us
    unnamed x4, local copies, waits for them, and re-layouts  10.3 us

profile of v1, /device:TPU:9, one launch (start us, length us, event | category | flops | bytes accessed | tf_op | source)
XLA Modules:
  0.0 190.4 jit_solution(14148652689556404508)
XLA Ops:
  0.6 0.7 fusion.2
  1.3 0.1 eq.24
  1.5 0.6 convert_reduce_fusion
  2.1 0.1 reshape.46
  2.2 0.1 dynamic-slice_add_fusion
  2.3 0.8 select_reduce_fusion.incoming
  3.1 0.7 select_reduce_fusion.1.outgoing
  3.8 176.3 %exchange.1 = (f32[288,32,128]{2,1,0:T(8,128)S(1)}, f32[288,32,128]{2,1,0:T(8,128)S(1)}, f32[288,32,128]{2,1,0:T(8,128)S(1)}, bf16[288,128,128]{2,1,0:T(8,128)(2,1)S(1)}) custom-call(s32[288]{0:T(512)} %select_reduce_fusion.1.outgoing, s32[288]{0:T(512)} %select_reduce_fusion.incoming, f32[288,32,128]{2,1,0:T(8,128)} %weight.1, f32[288,32,128]{2,1,0:T(8,128)} %first.1, ...), custom_call_target="tpu_custom_call" | custom-call | tf_op jit(solution)/shard_map/exchange/pallas_call | solution.py:301
  180.1 2.2 %copy.13 = f32[288,32,128]{2,1,0:T(8,128)} copy(f32[288,32,128]{2,1,0:T(8,128)S(1)} %get-tuple-element.6) | data formatting | bytes 9437184
  182.3 2.2 %copy.14 = f32[288,32,128]{2,1,0:T(8,128)} copy(f32[288,32,128]{2,1,0:T(8,128)S(1)} %get-tuple-element.7) | data formatting | bytes 9437184
  184.5 2.2 %copy.15 = f32[288,32,128]{2,1,0:T(8,128)} copy(f32[288,32,128]{2,1,0:T(8,128)S(1)} %get-tuple-element.8) | data formatting | bytes 9437184
  186.7 3.7 %copy.16 = bf16[288,128,128]{2,1,0:T(8,128)(2,1)} copy(bf16[288,128,128]{2,1,0:T(8,128)(2,1)S(1)} %get-tuple-element.9) | data formatting | bytes 18874368
  (2 shorter events, 0.0 us)

commit v2 on v1

--- a/solution.py
+++ b/solution.py
@@ -82,7 +82,7 @@
     parts = PARTS if slots % PARTS == 0 else 1
     me = lax.axis_index("tensor")
     mine = lax.axis_index("dp")
-    hops = sorted(range(1, groups), key=lambda k: -min(k, groups - k))
+    hops = range(1, groups)
     turns = range(1, replicas)
 
     def band(chunk, owner=None):
@@ -174,7 +174,15 @@
             copy.wait()
 
     def partner(k):
-        return lax.rem(me + k, groups)
+        if groups & (groups - 1):
+            return lax.rem(me + k, groups)
+        there = me
+        for bit in (1 << n for n in range(k.bit_length())):
+            if k & bit:
+                there = there + bit - 2 * bit * lax.rem(there // bit, 2)
+        return there
+
+    inner = (me > 0) & (me < groups - 1)
 
     def peer(k):
         return lax.rem(mine + k, replicas)
@@ -213,20 +221,27 @@
 
             lax.fori_loop(0, capacity, one, 0, unroll=math.gcd(capacity, 8))
 
-        waiting = None
+        def send(k, chunk=chunk):
+            if k == 1:
+                wide(chunk, me, partner(k)).start()
+            elif k > 1:
+                pl.when(inner)(lambda: wide(chunk, me, partner(k)).start())
+
         for k in hops:
             pack(partner(k))
-            if waiting is not None:
-                waiting.start()
-            waiting = wide(chunk, me, partner(k))
+            send(k - 1)
         pack(me)
-        if waiting is not None:
-            waiting.start()
+        send(groups - 1)
         if chunk + 2 < chunks:
             start(loads(chunk + 2))
         own(chunk).start()
         start([grad_copy(chunk, mine, peer(k)) for k in turns])
         grad_here(chunk).start()
+
+    @pl.when(jnp.logical_not(inner))
+    def _():
+        for chunk in range(chunks):
+            start([wide(chunk, me, partner(k)) for k in hops if k > 1])
 
     for chunk in range(chunks):
         grad_here(chunk).wait()

time: 191 us -> 191 us (level)
  no operation moved by 1% of the time
where the time goes in v2:
time: 191 us
  Pallas kernels  177 us (93%)
  local copies, waits for them, and re-layouts  10.5 us (5%)
  other arithmetic  3.03 us (2%)
    pallas_call x1, Pallas kernels, exchange(): pl.pallas_call(functools.partial(exchange_kernel, groups, replicas, capac...  177 us
    unnamed x4, local copies, waits for them, and re-layouts  10.3 us

profile of v2, /device:TPU:9, one launch (start us, length us, event | category | flops | bytes accessed | tf_op | source)
XLA Modules:
  0.0 190.7 jit_solution(14378645460726161402)
XLA Ops:
  0.6 0.7 fusion.2
  1.3 0.1 eq.24
  1.5 0.6 convert_reduce_fusion
  2.1 0.1 reshape.46
  2.2 0.1 dynamic-slice_add_fusion
  2.3 0.8 select_reduce_fusion.incoming
  3.1 0.7 select_reduce_fusion.1.outgoing
  3.8 176.5 %exchange.1 = (f32[288,32,128]{2,1,0:T(8,128)S(1)}, f32[288,32,128]{2,1,0:T(8,128)S(1)}, f32[288,32,128]{2,1,0:T(8,128)S(1)}, bf16[288,128,128]{2,1,0:T(8,128)(2,1)S(1)}) custom-call(s32[288]{0:T(512)} %select_reduce_fusion.1.outgoing, s32[288]{0:T(512)} %select_reduce_fusion.incoming, f32[288,32,128]{2,1,0:T(8,128)} %weight.1, f32[288,32,128]{2,1,0:T(8,128)} %first.1, ...), custom_call_target="tpu_custom_call" | custom-call | tf_op jit(solution)/shard_map/exchange/pallas_call | solution.py:316
  180.4 2.2 %copy.13 = f32[288,32,128]{2,1,0:T(8,128)} copy(f32[288,32,128]{2,1,0:T(8,128)S(1)} %get-tuple-element.6) | data formatting | bytes 9437184
  182.6 2.2 %copy.14 = f32[288,32,128]{2,1,0:T(8,128)} copy(f32[288,32,128]{2,1,0:T(8,128)S(1)} %get-tuple-element.7) | data formatting | bytes 9437184
  184.8 2.2 %copy.15 = f32[288,32,128]{2,1,0:T(8,128)} copy(f32[288,32,128]{2,1,0:T(8,128)S(1)} %get-tuple-element.8) | data formatting | bytes 9437184
  186.9 3.7 %copy.16 = bf16[288,128,128]{2,1,0:T(8,128)(2,1)} copy(bf16[288,128,128]{2,1,0:T(8,128)(2,1)S(1)} %get-tuple-element.9) | data formatting | bytes 18874368
  (2 shorter events, 0.0 us)
